TPU v7x, 256 devices: a whole 4x4x8 slice. The times are simulated.
256 devices in a mesh: dp: 4 (over x), expert: 64 (over z, y, core).
Axes of the slice: x: 4, y: 4, z: 8, core: 2. Of those that a mesh axis runs over, the one named last changes fastest.
Arguments:
- tokens: bfloat16 [32768, 1024], P(('dp', 'expert')), may hold values from -6 to 6
- routes: int32 [32768, 8], P(('dp', 'expert')), may hold values from 0 to 127, all different within a row; in each aligned block of 128 rows (0 to 127, 128 to 255, ...) at most 12 rows name the same one
- gates: float32 [32768, 8], P(('dp', 'expert')), may hold values from 0.05 to 0.5
- cotangent: bfloat16 [32768, 1024], P(('dp', 'expert')), may hold values from -6 to 6
- partner: int32 [128], replicated, may hold values from 0 to 127, as said below
- w_gate_up: bfloat16 [128, 1024, 768], P('expert'), may hold values from -0.1875 to 0.1875
- w_down: bfloat16 [128, 1024, 384], P('expert'), may hold values from -0.3125 to 0.3125
Outputs:
- mixed: bfloat16 [32768, 1024], P(('dp', 'expert'))
- grad_tokens: bfloat16 [32768, 1024], P(('dp', 'expert'))
- grad_gate_up: float32 [128, 1024, 768], P('expert', 'dp')
- grad_down: float32 [128, 1024, 384], P('expert', 'dp')
Inputs may be any that keep to these rules, and one draw needn't show every extreme that they name: `routes`: A token names 8 different experts. In each device's block of 128 consecutive tokens no expert is named by more than 12 tokens, a bound that some block reaches. partner is a permutation that is its own inverse: each slot either keeps its expert or trades it with one slot of the device half the expert axis away (slot s lies on index s // 2 of the expert axis); each device trades at most one of its slots, and some slots trade in every draw.
All inputs are finite; a program needn't handle non-finite values.
Results may differ from a plain program's by a relative error of at most 0.01.
Values may be sent and summed in bfloat16 or wider, within the bound.
A program may use at most 128 MiB of HBM per device.

v0:
```python
import jax
import jax.numpy as jnp
from jax import lax
from jax.sharding import PartitionSpec as P

grad_scale = 0.0625


def partner_2(block, axis, distance):
    count = lax.axis_size(axis)
    route = []
    for low in range(count):
        high = low | 1 << distance
        if high != low and high < count:
            route += [(low, high), (high, low)]
    return lax.ppermute(block, axis, route)


def table_lookup(table, keys):
    hits = keys[..., None] == jnp.arange(table.shape[0], dtype=jnp.int32)
    return jnp.sum(jnp.where(hits, table, 0), axis=-1)


def pick_slots(own_slots, received, moved, source_local):
    slots = own_slots.shape[0]
    index = jnp.where(moved, slots + source_local, jnp.arange(slots, dtype=jnp.int32))
    stacked = jnp.concatenate([own_slots, received], axis=0)
    return jnp.take(stacked, index, axis=0)


def local(tokens, routes, gates, cotangent, partner, w_gate_up, w_down):
    count_tokens, top_k = routes.shape
    width = tokens.shape[1]
    hidden_units = w_down.shape[2]
    n_expert = lax.axis_size("expert")
    exp_slots = w_gate_up.shape[0]
    experts_all = n_expert * exp_slots
    capacity = 3 * count_tokens * top_k // (2 * experts_all)
    pair_bit = n_expert.bit_length() - 2
    my_index = lax.axis_index("expert")
    slot_ids = my_index * exp_slots + jnp.arange(exp_slots, dtype=jnp.int32)
    partner_of = table_lookup(partner, slot_ids)
    moved = partner_of // exp_slots != my_index
    source_local = partner_of % exp_slots
    packed = jnp.concatenate([w_gate_up, w_down], axis=-1)
    target = table_lookup(partner, routes)
    received = partner_2(packed, "expert", pair_bit)
    packed = pick_slots(packed, received, moved, source_local)
    weight_gu = packed[:, :, : 2 * hidden_units]
    weight_dn = packed[:, :, 2 * hidden_units :]
    assign_total = count_tokens * top_k
    flat_slots = target.reshape(-1)
    hits = (flat_slots[:, None] == jnp.arange(experts_all, dtype=jnp.int32)).astype(jnp.int32)
    ranked = jnp.sum(jnp.cumsum(hits, axis=0) * hits, axis=1) - 1
    position = flat_slots * capacity + ranked
    filler = (
        jnp.full((experts_all * capacity,), assign_total, jnp.int32)
        .at[position]
        .set(jnp.arange(assign_total, dtype=jnp.int32))
    )
    buffer_shape = (n_expert, exp_slots, capacity, width)
    token_pad = jnp.concatenate([tokens, jnp.zeros((1, width), tokens.dtype)], axis=0)
    sending_rows = token_pad[filler // top_k].reshape(buffer_shape)
    arrived = lax.all_to_all(sending_rows, "expert", split_axis=0, concat_axis=0, tiled=True)
    pre_act = jnp.einsum("sjcd,jdf->sjcf", arrived, weight_gu, preferred_element_type=jnp.float32)
    gate_pre = pre_act[..., :hidden_units]
    up_pre = pre_act[..., hidden_units:]
    sigmoid_gate = jax.nn.sigmoid(gate_pre)
    silu_gate = gate_pre * sigmoid_gate
    hidden = (silu_gate * up_pre).astype(jnp.bfloat16)
    expert_out = jnp.einsum(
        "sjcf,jdf->sjcd", hidden, weight_dn, preferred_element_type=jnp.float32
    ).astype(jnp.bfloat16)
    returned = lax.all_to_all(expert_out, "expert", split_axis=0, concat_axis=0, tiled=True)
    picked = returned.reshape(-1, width)[position].reshape(count_tokens, top_k, width)
    mixed = jnp.einsum("tk,tkd->td", gates, picked.astype(jnp.float32)).astype(jnp.bfloat16)
    grad_out = (
        (gates[:, :, None] * cotangent[:, None, :].astype(jnp.float32))
        .astype(jnp.bfloat16)
        .reshape(assign_total, width)
    )
    grad_pad = jnp.concatenate([grad_out, jnp.zeros((1, width), jnp.bfloat16)], axis=0)
    grad_arrived = lax.all_to_all(
        grad_pad[filler].reshape(buffer_shape), "expert", split_axis=0, concat_axis=0, tiled=True
    )
    grad_hidden = jnp.einsum(
        "sjcd,jdf->sjcf", grad_arrived, weight_dn, preferred_element_type=jnp.float32
    )
    grad_down = jnp.einsum(
        "sjcf,sjcd->jdf", hidden, grad_arrived, preferred_element_type=jnp.float32
    )
    grad_gate = grad_hidden * up_pre * sigmoid_gate * (1.0 + gate_pre * (1.0 - sigmoid_gate))
    grad_up = grad_hidden * silu_gate
    grad_pre = jnp.concatenate([grad_gate, grad_up], axis=-1).astype(jnp.bfloat16)
    grad_rows = jnp.einsum(
        "sjcf,jdf->sjcd", grad_pre, weight_gu, preferred_element_type=jnp.float32
    ).astype(jnp.bfloat16)
    grad_gu = jnp.einsum("sjcd,sjcf->jdf", arrived, grad_pre, preferred_element_type=jnp.float32)
    grad_back = lax.all_to_all(grad_rows, "expert", split_axis=0, concat_axis=0, tiled=True)
    gathered = grad_back.reshape(-1, width)[position].reshape(count_tokens, top_k, width)
    grad_tokens = jnp.sum(gathered.astype(jnp.float32), axis=1).astype(jnp.bfloat16)
    terms = jnp.concatenate([grad_gu, grad_down], axis=-1) * grad_scale
    reduced = lax.psum_scatter(terms, "dp", scatter_dimension=1, tiled=True)
    return (
        mixed,
        grad_tokens,
        reduced[:, :, : 2 * hidden_units],
        reduced[:, :, 2 * hidden_units :],
    )


def solution(mesh):
    in_specs = (
        P(("dp", "expert"), None),
        P(("dp", "expert"), None),
        P(("dp", "expert"), None),
        P(("dp", "expert"), None),
        P(),
        P("expert", None, None),
        P("expert", None, None),
    )
    out_specs = (
        P(("dp", "expert"), None),
        P(("dp", "expert"), None),
        P("expert", "dp", None),
        P("expert", "dp", None),
    )
    return jax.shard_map(local, mesh=mesh, in_specs=in_specs, out_specs=out_specs, check_vma=False)
```

profile of v0, /device:TPU:2, one launch (start us, length us, event | category | flops | bytes accessed | tf_op | source)
XLA Modules:
  0.0 630.7 jit_solution(7342218311732798506)
XLA Ops:
  7.2 0.8 copy.52
  8.0 3.0 select_reduce_fusion
  12.3 4.3 scatter_custom_fusion
  16.7 5.1 gather_fusion
  21.7 2.7 reshape.186
  24.4 7.2 %copy.55 = bf16[64,2,12,1024]{3,1,2,0:T(2,128)(2,1)} copy(bf16[64,2,12,1024]{3,2,1,0:T(8,128)(2,1)} %reshape.186) | data formatting | bytes 6291456 | tf_op jit(solution)/shard_map/reshape | solution.py:63
  31.6 12.6 %all-to-all-start = ((bf16[64,2,12,1024]{3,1,2,0:T(2,128)(2,1)}), bf16[64,2,12,1024]{3,1,2,0:T(2,128)(2,1)}, u32[]{:S(2)}, u32[]{:S(2)}) async-start(bf16[64,2,12,1024]{3,1,2,0:T(2,128)(2,1)} %copy.55), calls=%async_computation | async-start | bytes 6291456 | tf_op jit(solution)/shard_map/all_to_all | solution.py:64
  44.2 1.9 constant_dynamic-update-slice_fusion.1
  46.3 1.4 constant_dynamic-update-slice_fusion
  47.6 5.7 collective-permute-start
  54.0 5.8 gather_fusion.2
  59.8 6.1 reshape.189
  65.9 7.2 %copy.60 = bf16[64,2,12,1024]{3,1,2,0:T(2,128)(2,1)} copy(bf16[64,2,12,1024]{3,2,1,0:T(8,128)(2,1)} %reshape.189) | data formatting | bytes 6291456 | tf_op jit(solution)/shard_map/reshape | solution.py:84
  73.1 44.2 %all-to-all-done = bf16[64,2,12,1024]{3,1,2,0:T(2,128)(2,1)} async-done(((bf16[64,2,12,1024]{3,1,2,0:T(2,128)(2,1)}), bf16[64,2,12,1024]{3,1,2,0:T(2,128)(2,1)}, u32[]{:S(2)}, u32[]{:S(2)}) %all-to-all-start) | async-done | bytes 3145760 | tf_op jit(solution)/shard_map/all_to_all | solution.py:64
  117.3 207.8 %all-to-all-start.2 = ((bf16[64,2,12,1024]{3,1,2,0:T(2,128)(2,1)}), bf16[64,2,12,1024]{3,1,2,0:T(2,128)(2,1)S(1)}, u32[]{:S(2)}, u32[]{:S(2)}) async-start(bf16[64,2,12,1024]{3,1,2,0:T(2,128)(2,1)} %copy.60), calls=%async_computation.2 | async-start | bytes 6291456 | tf_op jit(solution)/shard_map/all_to_all | solution.py:83
  325.4 4.5 pad_maximum_fusion
  329.9 4.2 gather_fusion.5
  334.0 6.0 fusion
  340.0 4.9 gather_fusion.4
  345.0 3.4 maximum_select_fusion
  348.4 2.1 copy-done
  350.5 8.0 %fusion.19 = f32[64,2,12,768]{3,0,2,1:T(8,128)} fusion(bf16[64,2,12,1024]{3,1,2,0:T(2,128)(2,1)} %all-to-all-done, bf16[2,1024,1152]{2,1,0:T(8,128)(2,1)S(1)} %maximum_select_fusion), kind=kOutput, calls=%fused_computation.38 | convolution fusion | flops 2415919104 | bytes 11010048 | tf_op jit(solution)/shard_map/sjcd,jdf->sjcf/dot_general | solution.py:65
  358.5 40.4 %all-to-all-done.2 = bf16[64,2,12,1024]{3,1,2,0:T(2,128)(2,1)S(1)} async-done(((bf16[64,2,12,1024]{3,1,2,0:T(2,128)(2,1)}), bf16[64,2,12,1024]{3,1,2,0:T(2,128)(2,1)S(1)}, u32[]{:S(2)}, u32[]{:S(2)}) %all-to-all-start.2) | async-done | bytes 3145760 | tf_op jit(solution)/shard_map/all_to_all | solution.py:83
  398.9 6.6 %fusion.16 = (bf16[64,2,12,384]{3,0,2,1:T(8,128)(2,1)S(1)}, bf16[64,2,12,384]{3,0,2,1:T(8,128)(2,1)S(1)}, bf16[64,2,12,384]{3,0,2,1:T(8,128)(2,1)S(1)}) fusion(f32[64,2,12,768]{3,0,2,1:T(8,128)} %fusion.19, bf16[64,2,12,1024]{3,1,2,0:T(2,128)(2,1)S(1)} %all-to-all-done.2, bf16[2,1024,1152]{2,1,0:T(8,128)(2,1)} %copy-done), kind=kOutput, calls=%fused_computation.33 | convolution fusion | flops 1216806912 | bytes 12976128 | tf_op jit(solution)/shard_map/sjcd,jdf->sjcf/dot_general | solution.py:86
  405.5 4.0 fusion.24
  409.6 14.3 %fusion.10 = f32[2,1024,768]{1,2,0:T(8,128)} fusion(bf16[64,2,12,1024]{3,1,2,0:T(2,128)(2,1)} %all-to-all-done, bf16[64,2,12,384]{3,0,2,1:T(8,128)(2,1)S(1)} %get-tuple-element.25, bf16[64,2,12,384]{3,0,2,1:T(8,128)(2,1)S(1)} %get-tuple-element.24), kind=kOutput, calls=%fused_computation.26 | convolution fusion | flops 2420637696 | bytes 11796480 | tf_op jit(solution)/shard_map/sjcd,sjcf->jdf/dot_general | solution.py:98
  423.9 8.3 %maximum_multiply_fusion = f32[2,1024,1152]{1,2,0:T(8,128)} fusion(f32[2,1024,384]{1,2,0:T(8,128)S(1)} %fusion.24, f32[2,1024,768]{1,2,0:T(8,128)} %fusion.10), kind=kLoop, calls=%fused_computation.9 | loop fusion | flops 4718592 | bytes 18874368 | tf_op jit(solution)/shard_map/mul | solution.py:102
  432.1 1.2 copy-done.4
  433.4 3.2 convert_bitcast_fusion.1
  436.6 4.9 copy.57
  441.6 5.7 all-to-all-start.1
  447.2 5.2 convert_bitcast_fusion
  452.5 4.9 copy.62
  457.4 63.5 %all-to-all-done.1 = bf16[64,2,12,1024]{3,1,2,0:T(2,128)(2,1)S(1)} async-done(((bf16[64,2,12,1024]{3,1,2,0:T(2,128)(2,1)}), bf16[64,2,12,1024]{3,1,2,0:T(2,128)(2,1)S(1)}, u32[]{:S(2)}, u32[]{:S(2)}) %all-to-all-start.1) | async-done | bytes 3145760 | tf_op jit(solution)/shard_map/all_to_all | solution.py:74
  520.9 5.8 all-to-all-start.3
  526.9 3.3 copy.58
  530.2 4.7 reshape.187
  534.9 5.3 gather_fusion.1
  540.3 2.3 fusion.22
  542.5 0.8 copy.91
  543.3 57.2 %all-to-all-done.3 = bf16[64,2,12,1024]{3,1,2,0:T(2,128)(2,1)} async-done(((bf16[64,2,12,1024]{3,1,2,0:T(2,128)(2,1)}), bf16[64,2,12,1024]{3,1,2,0:T(2,128)(2,1)}, u32[]{:S(2)}, u32[]{:S(2)}) %all-to-all-start.3) | async-done | bytes 3145760 | tf_op jit(solution)/shard_map/all_to_all | solution.py:99
  600.5 5.1 copy.63
  605.7 4.7 reshape.190
  610.4 5.3 gather_fusion.3
  615.7 3.7 bitcast_reduce_fusion
  619.5 1.4 slice-done
  620.9 1.6 copy.66
  622.5 1.1 copy.67
  (57 shorter events, 2.5 us)
Async XLA Ops:
  7.2 9.4 %copy-start.6 = (bf16[128,1024]{1,0:T(8,128)(2,1)S(1)}, bf16[128,1024]{1,0:T(8,128)(2,1)}, u32[]{:S(2)}) copy-start(bf16[128,1024]{1,0:T(8,128)(2,1)} %param.7) | copy-start | bytes 786436
  31.6 12.6 %copy-start.1 = (bf16[2,1024,768]{2,1,0:T(8,128)(2,1)S(1)}, bf16[2,1024,768]{2,1,0:T(8,128)(2,1)}, u32[]{:S(2)}) copy-start(bf16[2,1024,768]{2,1,0:T(8,128)(2,1)} %param.12) | copy-start | bytes 9437188
  31.6 85.7 %all-to-all-start = ((bf16[64,2,12,1024]{3,1,2,0:T(2,128)(2,1)}), bf16[64,2,12,1024]{3,1,2,0:T(2,128)(2,1)}, u32[]{:S(2)}, u32[]{:S(2)}) async-start(bf16[64,2,12,1024]{3,1,2,0:T(2,128)(2,1)} %copy.55), calls=%async_computation | async-start | bytes 6291456 | tf_op jit(solution)/shard_map/all_to_all | solution.py:64
  44.2 2.0 copy-start.2
  46.3 7.0 %copy-start.5 = (bf16[128,1024]{1,0:T(8,128)(2,1)S(1)}, bf16[128,1024]{1,0:T(8,128)(2,1)}, u32[]{:S(2)}) copy-start(bf16[128,1024]{1,0:T(8,128)(2,1)} %param.10) | copy-start | bytes 786436
  46.3 7.1 %copy-start.7 = (f32[128,8]{0,1:T(8,128)S(1)}, f32[128,8]{0,1:T(8,128)}, u32[]{:S(2)}) copy-start(f32[128,8]{0,1:T(8,128)} %param.9) | copy-start | bytes 12292
  47.6 277.7 %collective-permute-start = (bf16[2,1024,1152]{2,1,0:T(8,128)(2,1)}, bf16[2,1024,1152]{2,1,0:T(8,128)(2,1)}, u32[]{:S(2)}, u32[]{:S(2)}) collective-permute-start(bf16[2,1024,1152]{2,1,0:T(8,128)(2,1)} %constant_dynamic-update-slice_fusion), channel_id=1, source_target_pairs={{0,32},{32,0},{1,33},{33,1},{2,34},{34,2},{3,35},{35,3},{4,36},{36... | collective-permute-start | bytes 14155784 | tf_op jit(solution)/shard_map/ppermute | solution.py:16
  73.1 252.0 %copy-start.8 = (s32[128]{0:T(128)S(1)}, s32[128]{0:T(128)}, u32[]{:S(2)}) copy-start(s32[128]{0:T(128)} %param.11) | copy-start | bytes 1540
  117.3 281.6 %all-to-all-start.2 = ((bf16[64,2,12,1024]{3,1,2,0:T(2,128)(2,1)}), bf16[64,2,12,1024]{3,1,2,0:T(2,128)(2,1)S(1)}, u32[]{:S(2)}, u32[]{:S(2)}) async-start(bf16[64,2,12,1024]{3,1,2,0:T(2,128)(2,1)} %copy.60), calls=%async_computation.2 | async-start | bytes 6291456 | tf_op jit(solution)/shard_map/all_to_all | solution.py:83
  325.0 294.4 %reduce-scatter.2.cloned.1.call-start = ((), (), s32[]{:S(2)}) async-start(), calls=%async_computation.5 | async-start | bytes 11796480 | tf_op jit(solution)/shard_map/reduce_scatter | solution.py:103
  348.4 2.1 copy-start
  405.5 4.1 copy-start.3
  405.5 4.1 copy-start.9
  405.5 4.1 copy-start.10
  432.1 1.3 copy-start.4
  441.6 79.4 %all-to-all-start.1 = ((bf16[64,2,12,1024]{3,1,2,0:T(2,128)(2,1)}), bf16[64,2,12,1024]{3,1,2,0:T(2,128)(2,1)S(1)}, u32[]{:S(2)}, u32[]{:S(2)}) async-start(bf16[64,2,12,1024]{3,1,2,0:T(2,128)(2,1)} %copy.57), calls=%async_computation.1 | async-start | bytes 6291456 | tf_op jit(solution)/shard_map/all_to_all | solution.py:74
  520.9 79.6 %all-to-all-start.3 = ((bf16[64,2,12,1024]{3,1,2,0:T(2,128)(2,1)}), bf16[64,2,12,1024]{3,1,2,0:T(2,128)(2,1)}, u32[]{:S(2)}, u32[]{:S(2)}) async-start(bf16[64,2,12,1024]{3,1,2,0:T(2,128)(2,1)} %copy.62), calls=%async_computation.3 | async-start | bytes 6291456 | tf_op jit(solution)/shard_map/all_to_all | solution.py:99
  619.5 1.4 slice-start
  620.9 1.6 slice-start.1
Sparse Core Ops, SparseCore 0:
  432.3 86.4 reduce-scatter.1
where the time goes:
time: 639 us; the launch traced here: 631 us
  starting transfers between devices  238 us (37%)
  waiting for transfers between devices  205 us (32%)
  local copies, waits for them, and re-layouts  99.3 us (16%)
  matrix products  43.6 us (7%)
  other arithmetic  30.2 us (5%)
  between operations  14.6 us (2%)
    all_to_all x1, starting transfers between devices, local(): lax.all_to_all(grad_pad[filler].reshape(buffer_shape), 'expert', split_ax...  208 us
    all_to_all x1, waiting for transfers between devices, local(): lax.all_to_all(expert_out, 'expert', split_axis=0, concat_axis=0, tiled=T...  63.5 us
    all_to_all x1, waiting for transfers between devices, local(): lax.all_to_all(grad_rows, 'expert', split_axis=0, concat_axis=0, tiled=True)  57.2 us
    all_to_all x1, waiting for transfers between devices, local(): lax.all_to_all(sending_rows, 'expert', split_axis=0, concat_axis=0, tiled...  44.2 us
    all_to_all x1, waiting for transfers between devices, local(): lax.all_to_all(grad_pad[filler].reshape(buffer_shape), 'expert', split_ax...  40.4 us
    dot_general x1, matrix products, local(): jnp.einsum('sjcd,sjcf->jdf', arrived, grad_pre, preferred_element_type=jn...  14.3 us
    reshape x2, local copies, waits for them, and re-layouts, local(): grad_pad[filler].reshape(buffer_shape)  13.2 us
  transfers between devices with their start and end apart: 6, of which 4 were waited for; matrix products, arithmetic and copies ran while one was open for 17% of the time, Pallas kernels for 0%

commit v1 on v0

v1 whole, which is shorter than its diff:
```python
import functools

import jax
import jax.numpy as jnp
import numpy as np
from jax import lax
from jax.experimental import pallas as pl
from jax.experimental.pallas import tpu as pltpu
from jax.sharding import PartitionSpec as P

MESH = pl.DeviceIdType.MESH
bf16, f32 = jnp.bfloat16, jnp.float32

grad_scale = 0.0625
PLANE = 8
CAP = 12
BLOCKS = 4
ROWS = CAP * BLOCKS
GROUPS = ((0, 1, -1, -2), (2, 3, -3, 4))
PLACE = {offset: (g, b) for g, group in enumerate(GROUPS) for b, offset in enumerate(group)}


def dot_nn(a, b):
    return lax.dot_general(a, b, (((1,), (0,)), ((), ())), preferred_element_type=f32)


def dot_nt(a, b):
    return lax.dot_general(a, b, (((1,), (1,)), ((), ())), preferred_element_type=f32)


def dot_tn(a, b):
    return lax.dot_general(a, b, (((0,), (0,)), ((), ())), preferred_element_type=f32)


def places():
    dp, index = lax.axis_index("dp"), lax.axis_index("expert")
    n_dp, n_z = lax.axis_size("dp"), lax.axis_size("expert") // PLANE
    return dp, index // PLANE, index % PLANE, n_dp, n_z


def remote(src, dst, send, recv, device):
    return pltpu.make_async_remote_copy(
        src_ref=src, dst_ref=dst, send_sem=send, recv_sem=recv, device_id=device, device_id_type=MESH
    )


def greet(devices):
    barrier = pltpu.get_barrier_semaphore()
    for device in devices:
        pl.semaphore_signal(barrier, inc=1, device_id=device, device_id_type=MESH)
    pl.semaphore_wait(barrier, len(devices))


def dispatch_kernel(
    tokens, cot, routes_t, gates_t, partner, expand, wanted, ws_gu, ws_dn,
    got_t, got_c, pick, pick_gate, wr_gu, wr_dn,
    xt, xc, rg, out_t, out_c,
    t_send, t_recv, c_send, c_recv, r_send, r_recv, y_send, y_recv, l_sem, w_send, w_recv, x_send, x_recv,
):
    dp, z, yc, n_dp, n_z = places()

    def at_z(shift):
        return (dp, lax.rem(z + shift + n_z, n_z) * PLANE + yc)

    def at_yc(shift):
        return (dp, z * PLANE + lax.rem(yc + shift, PLANE))

    def at_x(shift):
        return (lax.rem(dp + shift, n_dp), z * PLANE + yc)

    half = n_z // 2
    greet(
        [at_z(1), at_z(-1), at_z(half)]
        + [at_yc(i) for i in range(1, PLANE)]
        + [at_x(i) for i in range(1, 4)]
    )

    hops = [(k - 1, k, -1) for k in range(1, 5)] + [(1 - k, -k, 1) for k in range(1, 4)]

    def hop(buf, first, send, recv, number):
        here, there, way = hops[number]
        g, b = PLACE[there]
        source = first if here == 0 else buf.at[PLACE[here][0], PLACE[here][1]]
        return remote(source, buf.at[g, b], send.at[number], recv.at[number], at_z(way))

    t_hop = functools.partial(hop, xt, tokens, t_send, t_recv)
    c_hop = functools.partial(hop, xc, cot, c_send, c_recv)
    r_hop = functools.partial(hop, rg, rg.at[0, 0], r_send, r_recv)

    t_hop(0).start()
    t_hop(4).start()

    n_slots, count = rg.shape[2] // 2, rg.shape[3]
    row = lax.broadcasted_iota(jnp.int32, (n_slots, count), 0)
    col = lax.broadcasted_iota(jnp.int32, (n_slots, count), 1)
    named = jnp.zeros((n_slots, count), f32)
    weight = jnp.zeros((n_slots, count), f32)
    for k in range(routes_t.shape[0]):
        hit = routes_t[k : k + 1, :] == row
        named = named + jnp.where(hit, 1.0, 0.0)
        weight = weight + jnp.where(hit, gates_t[k : k + 1, :], 0.0)
    to_slot = jnp.where(partner[...] == col, 1.0, 0.0).astype(bf16)
    named = dot_nn(to_slot, named.astype(bf16))
    weight = dot_nn(to_slot, weight.astype(bf16))
    upto = jnp.where(row <= col, 1.0, 0.0).astype(bf16)
    rank = named * dot_nn(named.astype(bf16), upto)
    rg[0, 0, :n_slots, :] = rank.astype(bf16)
    rg[0, 0, n_slots:, :] = weight.astype(bf16)
    r_hop(0).start()
    r_hop(4).start()
    xt[0, 0] = tokens[...]
    xc[0, 0] = cot[...]

    per_plane = n_slots // n_z

    def build(g):
        for b in range(BLOCKS):
            start = pl.multiple_of(z * per_plane, per_plane)
            ranks = rg[g, b, pl.ds(start, per_plane), :]
            gates = rg[g, b, pl.ds(n_slots + start, per_plane), :]
            hit = dot_nn(expand[...], ranks) == wanted[:, b : b + 1]
            spread = dot_nn(expand[...], gates)
            columns = slice(b * count, (b + 1) * count)
            pick[g, :, columns] = jnp.where(hit, 1.0, 0.0).astype(bf16)
            pick_gate[g, :, columns] = jnp.where(hit, spread, 0.0).astype(bf16)

    width = tokens.shape[1]
    tile = 256

    def gather(matrix, buf, out, g):
        m = matrix[g]
        for j in range(width // tile):
            columns = pl.ds(j * tile, tile)
            block = buf[g, :, :, columns].reshape(BLOCKS * count, tile)
            out[g, :, :, columns] = dot_nn(m, block).astype(bf16).reshape(PLANE, 2 * ROWS, tile)

    def y_copy(out, got, phase, i):
        g = phase % 2
        p = lax.rem(yc + i, PLANE)
        return remote(out.at[g, p], got.at[g * PLANE + yc], y_send.at[phase, i], y_recv.at[phase, i], at_yc(i))

    def y_local(out, got, phase):
        g = phase % 2
        return pltpu.make_async_copy(out.at[g, yc], got.at[g * PLANE + yc], l_sem.at[phase])

    def y_start(out, got, phase):
        for i in range(1, PLANE):
            y_copy(out, got, phase, i).start()
        y_local(out, got, phase).start()

    def both(number, *makers):
        for make in makers:
            make(number).wait_recv()

    for k in (1, 2):
        both(k - 1, t_hop, r_hop)
        both(k + 3, t_hop, r_hop)
        t_hop(k).start()
        r_hop(k).start()
        t_hop(k + 4).start()
        r_hop(k + 4).start()
    build(0)
    gather(pick, xt, out_t, 0)
    y_start(out_t, got_t, 0)
    both(2, t_hop, r_hop)
    t_hop(3).start()
    r_hop(3).start()
    c_hop(0).start()
    c_hop(4).start()

    quarter = ws_gu.shape[0]
    rows = pl.ds(pl.multiple_of(dp * quarter, quarter), quarter)
    pairs = ((ws_gu, wr_gu), (ws_dn, wr_dn))

    def w_copy(n):
        return remote(pairs[n][0], pairs[n][1].at[rows, :], w_send.at[n], w_recv.at[n], at_z(half))

    def x_copy(n, i):
        here = pairs[n][1].at[rows, :]
        return remote(here, here, x_send.at[n, i], x_recv.at[n, i], at_x(i))

    w_copy(0).start()
    w_copy(1).start()
    both(6, t_hop, r_hop)
    both(3, t_hop, r_hop)
    build(1)
    gather(pick, xt, out_t, 1)
    both(0, c_hop)
    both(4, c_hop)
    c_hop(1).start()
    c_hop(5).start()
    y_start(out_t, got_t, 1)
    both(1, c_hop)
    both(5, c_hop)
    c_hop(2).start()
    c_hop(6).start()
    gather(pick_gate, xc, out_c, 0)
    y_start(out_c, got_c, 2)
    both(2, c_hop)
    c_hop(3).start()
    for n in range(2):
        w_copy(n).wait_recv()
        for i in range(1, 4):
            x_copy(n, i).start()
    both(6, c_hop)
    both(3, c_hop)
    gather(pick_gate, xc, out_c, 1)
    y_start(out_c, got_c, 3)

    for number in range(7):
        for make in (t_hop, c_hop, r_hop):
            make(number).wait_send()
    for phase in range(4):
        out, got = ((out_t, got_t), (out_c, got_c))[phase // 2]
        for i in range(1, PLANE):
            copy = y_copy(out, got, phase, i)
            copy.wait_send()
            copy.wait_recv()
        y_local(out, got, phase).wait()
    for n in range(2):
        w_copy(n).wait_send()
        for i in range(1, 4):
            x_copy(n, i).wait_send()
            x_copy(n, i).wait_recv()


def dispatch(tokens, routes, gates, cotangent, partner, ws_gu, ws_dn, n_slots, n_dp):
    count, width = tokens.shape
    n_z = lax.axis_size("expert") // PLANE
    per_plane = n_slots // n_z
    picked = per_plane * ROWS
    number = np.arange(picked)
    expand = (number[:, None] // ROWS == np.arange(per_plane)[None, :]).astype(np.float32)
    wanted = np.where(
        number[:, None] % ROWS // CAP == np.arange(BLOCKS)[None, :], (number % CAP + 1)[:, None], -1
    ).astype(np.float32)
    vmem, hbm = pl.BlockSpec(memory_space=pltpu.VMEM), pl.BlockSpec(memory_space=pl.ANY)
    dma = pltpu.SemaphoreType.DMA
    slab = jax.ShapeDtypeStruct((2 * PLANE, 2 * ROWS, width), bf16)
    matrix = jax.ShapeDtypeStruct((2, picked, BLOCKS * count), bf16)
    return pl.pallas_call(
        dispatch_kernel,
        out_shape=(
            slab, slab, matrix, matrix,
            jax.ShapeDtypeStruct((n_dp * ws_gu.shape[0], ws_gu.shape[1]), bf16),
            jax.ShapeDtypeStruct((n_dp * ws_dn.shape[0], ws_dn.shape[1]), bf16),
        ),
        in_specs=[vmem] * 7 + [hbm] * 2,
        out_specs=(hbm, hbm, vmem, vmem, hbm, hbm),
        scratch_shapes=[
            pltpu.VMEM((2, BLOCKS, count, width), bf16),
            pltpu.VMEM((2, BLOCKS, count, width), bf16),
            pltpu.VMEM((2, BLOCKS, 2 * n_slots, count), bf16),
            pltpu.VMEM((2, PLANE, 2 * ROWS, width), bf16),
            pltpu.VMEM((2, PLANE, 2 * ROWS, width), bf16),
            dma((7,)), dma((7,)), dma((7,)), dma((7,)), dma((7,)), dma((7,)),
            dma((4, PLANE)), dma((4, PLANE)), dma((4,)),
            dma((2,)), dma((2,)), dma((2, 4)), dma((2, 4)),
        ],
        compiler_params=pltpu.CompilerParams(
            collective_id=0, has_side_effects=True, vmem_limit_bytes=48 << 20
        ),
        name="dispatch",
    )(
        tokens, cotangent, routes.T, gates.T, partner[:, None],
        jnp.asarray(expand, bf16), jnp.asarray(wanted), ws_gu, ws_dn,
    )


def expert_kernel(
    moved, xt, xc, w_gu, w_dn, wr_gu, wr_dn, yo, yg, g_gu, g_dn, gu, dn, hid, gpre, sem
):
    j = pl.program_id(0)
    width = xt.shape[3]
    ff = hid.shape[1]
    chunks = PLANE
    rows = chunks * ROWS

    def load(gu_src, dn_src):
        a = pltpu.make_async_copy(gu_src, gu, sem.at[0])
        b = pltpu.make_async_copy(dn_src, dn, sem.at[1])
        a.start()
        b.start()
        a.wait()
        b.wait()

    @pl.when(moved[j] == 0)
    def _():
        load(w_gu.at[j], w_dn.at[j])

    @pl.when(moved[j] != 0)
    def _():
        load(wr_gu, wr_dn)

    @pl.loop(0, 2)
    def _(i):
        part = pl.ds(i * chunks, chunks)
        here = pl.ds(pl.multiple_of(i * rows, rows), rows)
        x = xt[part, 0].reshape(rows, width)
        pre = dot_nn(x, gu[...])
        gate, up = pre[:, :ff], pre[:, ff:]
        sig = jax.nn.sigmoid(gate)
        silu = gate * sig
        hidden = (silu * up).astype(bf16)
        hid[here, :] = hidden
        yo[part, 0] = dot_nt(hidden, dn[...]).astype(bf16).reshape(chunks, ROWS, width)
        c = xc[part, 0].reshape(rows, width)
        grad = dot_nn(c, dn[...])
        grad_gate = grad * up * sig * (1.0 + gate * (1.0 - sig))
        gpre[here, :ff] = grad_gate.astype(bf16)
        gpre[here, ff:] = (grad * silu).astype(bf16)
        yg[part, 0] = dot_nt(gpre[here, :], gu[...]).astype(bf16).reshape(chunks, ROWS, width)

    tile = 256

    @pl.loop(0, width // tile)
    def _(i):
        columns = pl.ds(pl.multiple_of(i * tile, tile), tile)
        x = xt[:, 0, :, columns].reshape(2 * rows, tile)
        g_gu[0, columns, :] = (dot_tn(x, gpre[...]) * grad_scale).astype(bf16)
        c = xc[:, 0, :, columns].reshape(2 * rows, tile)
        g_dn[0, columns, :] = (dot_tn(c, hid[...]) * grad_scale).astype(bf16)


def experts(moved, got_t, got_c, w_gu, w_dn, wr_gu, wr_dn):
    slots, width, ff2 = w_gu.shape
    ff = ff2 // 2
    shape = (2 * PLANE, slots, ROWS, width)
    hbm = pl.BlockSpec(memory_space=pl.ANY)
    slab = pl.BlockSpec((2 * PLANE, 1, ROWS, width), lambda j, m: (0, j, 0, 0))
    flat = (2 * PLANE, slots * ROWS, width)
    outs = pl.pallas_call(
        expert_kernel,
        grid_spec=pltpu.PrefetchScalarGridSpec(
            num_scalar_prefetch=1,
            grid=(slots,),
            in_specs=[slab, slab, hbm, hbm, hbm, hbm],
            out_specs=(
                slab,
                slab,
                pl.BlockSpec((1, width, ff2), lambda j, m: (j, 0, 0)),
                pl.BlockSpec((1, width, ff), lambda j, m: (j, 0, 0)),
            ),
            scratch_shapes=[
                pltpu.VMEM((width, ff2), bf16),
                pltpu.VMEM((width, ff), bf16),
                pltpu.VMEM((2 * PLANE * ROWS, ff), bf16),
                pltpu.VMEM((2 * PLANE * ROWS, ff2), bf16),
                pltpu.SemaphoreType.DMA((2,)),
            ],
        ),
        out_shape=(
            jax.ShapeDtypeStruct(shape, bf16),
            jax.ShapeDtypeStruct(shape, bf16),
            jax.ShapeDtypeStruct((slots, width, ff2), bf16),
            jax.ShapeDtypeStruct((slots, width, ff), bf16),
        ),
        compiler_params=pltpu.CompilerParams(vmem_limit_bytes=56 << 20),
        name="experts",
    )(moved, got_t.reshape(shape), got_c.reshape(shape), w_gu, w_dn, wr_gu, wr_dn)
    return outs[0].reshape(flat), outs[1].reshape(flat), outs[2], outs[3]


def combine_kernel(
    yo, yg, pick, pick_gate, g_gu, g_dn,
    mixed, grad_tokens, xr_gu, xr_dn,
    ybuf, part, ring_in, ring_out,
    y_send, y_recv, l_sem, z_send, z_recv, x_send, x_recv,
):
    dp, z, yc, n_dp, n_z = places()

    def at_z(shift):
        return (dp, lax.rem(z + shift + n_z, n_z) * PLANE + yc)

    def at_yc(shift):
        return (dp, z * PLANE + lax.rem(yc + shift, PLANE))

    def at_x(shift):
        return (lax.rem(dp + shift, n_dp), z * PLANE + yc)

    greet(
        [at_z(1), at_z(-1)]
        + [at_yc(i) for i in range(1, PLANE)]
        + [at_x(i) for i in range(1, 4)]
    )

    def y_copy(phase, i):
        source, g = (yo, yg)[phase // 2], 1 - phase % 2
        p = lax.rem(yc + i, PLANE)
        return remote(
            source.at[g * PLANE + p], ybuf.at[phase, yc], y_send.at[phase, i], y_recv.at[phase, i], at_yc(i)
        )

    def y_local(phase):
        source, g = (yo, yg)[phase // 2], 1 - phase % 2
        return pltpu.make_async_copy(source.at[g * PLANE + yc], ybuf.at[phase, yc], l_sem.at[phase])

    def y_start(phase):
        for i in range(1, PLANE):
            y_copy(phase, i).start()
        y_local(phase).start()

    quarter = xr_gu.shape[2]
    pairs = ((g_gu, xr_gu), (g_dn, xr_dn))

    def x_copy(n, i):
        to = lax.rem(dp + i, n_dp)
        rows = pl.ds(pl.multiple_of(to * quarter, quarter), quarter)
        return remote(
            pairs[n][0].at[:, rows, :], pairs[n][1].at[i - 1], x_send.at[n, i], x_recv.at[n, i], at_x(i)
        )

    y_start(0)
    for n in range(2):
        for i in range(1, 4):
            x_copy(n, i).start()
    y_start(1)

    count, width = mixed.shape
    tile = 256

    def y_take(phase):
        for i in range(1, PLANE):
            y_copy(phase, i).wait_recv()
        y_local(phase).wait()
        stream, g = phase // 2, 1 - phase % 2
        matrix = (pick_gate, pick)[stream]
        for j in range(width // tile):
            columns = pl.ds(j * tile, tile)
            y = ybuf[phase, :, :, columns].reshape(PLANE * 2 * ROWS, tile)
            part[g, :, columns] = dot_tn(matrix[g], y)

    def own(offset):
        g, b = PLACE[offset]
        return part[g, b * count : (b + 1) * count, :]

    offsets = (3, 2, 1, 4, -3, -2, -1)

    def z_copy(stream, n):
        way = 1 if n < 3 else -1
        return remote(
            ring_out.at[stream, n], ring_in.at[stream, n], z_send.at[stream, n], z_recv.at[stream, n], at_z(way)
        )

    def z_step(stream, n):
        total = own(offsets[n])
        if n not in (0, 3):
            z_copy(stream, n - 1).wait_recv()
            total = total + ring_in[stream, n - 1].astype(f32)
        ring_out[stream, n] = total.astype(bf16)
        z_copy(stream, n).start()

    for stream in range(2):
        y_take(2 * stream)
        z_step(stream, 0)
        z_step(stream, 3)
        if stream == 0:
            y_start(2)
        z_step(stream, 1)
        z_step(stream, 4)
        y_take(2 * stream + 1)
        z_step(stream, 2)
        z_step(stream, 5)
        if stream == 0:
            y_start(3)
        z_step(stream, 6)
        z_copy(stream, 2).wait_recv()
        z_copy(stream, 6).wait_recv()
        total = own(0) + ring_in[stream, 2].astype(f32) + ring_in[stream, 6].astype(f32)
        (mixed, grad_tokens)[stream][...] = total.astype(bf16)

    for stream in range(2):
        for n in range(7):
            z_copy(stream, n).wait_send()
    for phase in range(4):
        for i in range(1, PLANE):
            y_copy(phase, i).wait_send()
    for n in range(2):
        for i in range(1, 4):
            x_copy(n, i).wait_send()
            x_copy(n, i).wait_recv()


def combine(yo, yg, pick, pick_gate, g_gu, g_dn, count, n_dp):
    slots, width, ff2 = g_gu.shape
    ff = ff2 // 2
    quarter = width // n_dp
    vmem, hbm = pl.BlockSpec(memory_space=pltpu.VMEM), pl.BlockSpec(memory_space=pl.ANY)
    dma = pltpu.SemaphoreType.DMA
    own = jax.ShapeDtypeStruct((count, width), bf16)
    return pl.pallas_call(
        combine_kernel,
        out_shape=(
            own, own,
            jax.ShapeDtypeStruct((n_dp - 1, slots, quarter, ff2), bf16),
            jax.ShapeDtypeStruct((n_dp - 1, slots, quarter, ff), bf16),
        ),
        in_specs=[hbm, hbm, vmem, vmem, hbm, hbm],
        out_specs=(vmem, vmem, hbm, hbm),
        scratch_shapes=[
            pltpu.VMEM((4, PLANE, 2 * ROWS, width), bf16),
            pltpu.VMEM((2, BLOCKS * count, width), f32),
            pltpu.VMEM((2, 7, count, width), bf16),
            pltpu.VMEM((2, 7, count, width), bf16),
            dma((4, PLANE)), dma((4, PLANE)), dma((4,)), dma((2, 7)), dma((2, 7)), dma((2, 4)), dma((2, 4)),
        ],
        compiler_params=pltpu.CompilerParams(
            collective_id=1, has_side_effects=True, vmem_limit_bytes=48 << 20
        ),
        name="combine",
    )(yo, yg, pick, pick_gate, g_gu, g_dn)


def local(tokens, routes, gates, cotangent, partner, w_gate_up, w_down):
    slots, width, ff2 = w_gate_up.shape
    n_dp, n_expert = lax.axis_size("dp"), lax.axis_size("expert")
    dp, index = lax.axis_index("dp"), lax.axis_index("expert")
    quarter = width // n_dp
    mine = lax.dynamic_slice(partner, (index * slots,), (slots,))
    moved = (mine // slots != index).astype(jnp.int32)
    going = jnp.argmax(moved).astype(jnp.int32)
    ws_gu = lax.dynamic_slice(w_gate_up, (going, dp * quarter, 0), (1, quarter, ff2))[0]
    ws_dn = lax.dynamic_slice(w_down, (going, dp * quarter, 0), (1, quarter, ff2 // 2))[0]
    got_t, got_c, pick, pick_gate, wr_gu, wr_dn = dispatch(
        tokens, routes, gates, cotangent, partner, ws_gu, ws_dn, n_expert * slots, n_dp
    )
    yo, yg, g_gu, g_dn = experts(moved, got_t, got_c, w_gate_up, w_down, wr_gu, wr_dn)
    mixed, grad_tokens, xr_gu, xr_dn = combine(
        yo, yg, pick, pick_gate, g_gu, g_dn, tokens.shape[0], n_dp
    )

    def total(own, others):
        own = lax.dynamic_slice(own, (0, dp * quarter, 0), (slots, quarter, own.shape[2]))
        return own.astype(f32) + jnp.sum(others.astype(f32), axis=0)

    return mixed, grad_tokens, total(g_gu, xr_gu), total(g_dn, xr_dn)


def solution(mesh):
    token_spec = P(("dp", "expert"), None)
    weight_spec = P("expert", None, None)
    grad_spec = P("expert", "dp", None)
    return jax.shard_map(
        local,
        mesh=mesh,
        in_specs=(token_spec, token_spec, token_spec, token_spec, P(None), weight_spec, weight_spec),
        out_specs=(token_spec, token_spec, grad_spec, grad_spec),
        check_vma=False,
    )
```

time: 639 us -> 251 us (0.39)
  starting transfers between devices: 238 us -> 0 us
  Pallas kernels: 0 us -> 227 us
  waiting for transfers between devices: 205 us -> 0 us
  local copies, waits for them, and re-layouts: 99.3 us -> 10.2 us
  matrix products: 43.6 us -> 0 us
  other arithmetic: 30.2 us -> 7.73 us
  between operations: 14.6 us -> 2.66 us
    all_to_all x4 -> x0, starting transfers between devices: 232 us -> none  [the longest x1 208 us: local(): lax.all_to_all(grad_pad[filler].reshape(buffer_shape), 'expert', split_ax...]
    pallas_call x0 -> x3, Pallas kernels: none -> 227 us  [the longest x1 110 us: dispatch(): pl.pallas_call(dispatch_kernel, out_shape=(slab, slab, matrix, matrix, ja...]
    all_to_all x4 -> x0, waiting for transfers between devices: 205 us -> none  [the longest x1 63.5 us: local(): lax.all_to_all(expert_out, 'expert', split_axis=0, concat_axis=0, tiled=T...]
    dot_general x7 -> x0, matrix products: 43.6 us -> none  [the longest x1 14.3 us: local(): jnp.einsum('sjcd,sjcf->jdf', arrived, grad_pre, preferred_element_type=jn...]
    reshape x6 -> x0, local copies, waits for them, and re-layouts: 32.5 us -> none  [the longest x2 13.2 us: local(): grad_pad[filler].reshape(buffer_shape)]
    gather x6 -> x0, local copies, waits for them, and re-layouts: 30.6 us -> none  [the longest x2 9.07 us: pick_slots(): return jnp.take(stacked, index, axis=0)]
    concatenate x2 -> x0, other arithmetic: 10.5 us -> none  [pick_slots(): stacked = jnp.concatenate([own_slots, received], axis=0)]
    convert_element_type x2 -> x0, local copies, waits for them, and re-layouts: 9.83 us -> none  [the longest x1 4.93 us: local(): expert_out = jnp.einsum('sjcf,jdf->sjcd', hidden, weight_dn, preferred_el...]
  transfers between devices with their start and end apart: 6 -> 0, of which waited for: 4 -> 0; matrix products, arithmetic and copies ran while one was open for 17% -> 0% of each run, Pallas kernels for 0% -> 0%
where the time goes in v1:
time: 251 us; the launch traced here: 247 us
  Pallas kernels  227 us (90%)
  local copies, waits for them, and re-layouts  10.2 us (4%)
  other arithmetic  7.73 us (3%)
  between operations  2.66 us (1%)
    pallas_call x1, Pallas kernels, dispatch(): pl.pallas_call(dispatch_kernel, out_shape=(slab, slab, matrix, matrix, ja...  110 us
    pallas_call x1, Pallas kernels, combine(): pl.pallas_call(combine_kernel, out_shape=(own, own, jax.ShapeDtypeStruct(...  89.7 us
    pallas_call x1, Pallas kernels, experts(): pl.pallas_call(expert_kernel, grid_spec=pltpu.PrefetchScalarGridSpec(num_...  27 us
    unnamed x18, local copies, waits for them, and re-layouts  7.47 us

profile of v1, /device:TPU:2, one launch (start us, length us, event | category | flops | bytes accessed | tf_op | source)
XLA Modules:
  0.0 247.4 jit_solution(10787488303078462673)
XLA Ops:
  0.6 1.2 compare_convert_fusion.moved
  1.9 1.4 iota_reduce_fusion
  5.2 0.8 copy.13.partner
  6.0 1.0 dynamic-slice_bitcast_fusion.1.ws_dn
  6.9 1.0 dynamic-slice_bitcast_fusion.ws_gu
  8.0 0.0 copy-start.1
  8.0 1.0 copy-done.1
  9.0 0.0 copy-start.2
  9.0 0.9 copy-done.2
  9.9 0.0 copy-start.3
  9.9 0.9 copy-done.3
  10.9 0.0 copy-start.4
  10.9 0.9 copy-done.4
  11.8 0.0 copy-start.5
  11.8 0.7 copy-done.5
  12.5 0.0 copy-start.6
  12.5 0.7 copy-done.6
  13.2 110.1 %dispatch.1 = (bf16[16,96,1024]{2,1,0:T(8,128)(2,1)}, bf16[16,96,1024]{2,1,0:T(8,128)(2,1)}, bf16[2,768,512]{2,1,0:T(8,128)(2,1)S(1)}, bf16[2,768,512]{2,1,0:T(8...) custom-call(bf16[128,1024]{1,0:T(8,128)(2,1)S(1)} %copy-done.2, ...), custom_call_target="tpu_custom_call" | custom-call | tf_op jit(solution)/shard_map/dispatch/pallas_call | solution.py:241
  123.3 0.0 copy-start
  123.3 0.9 copy-done
  124.2 27.0 %experts.1 = (bf16[16,2,48,1024]{3,2,1,0:T(8,128)(2,1)}, bf16[16,2,48,1024]{3,2,1,0:T(8,128)(2,1)}, bf16[2,1024,768]{2,1,0:T(8,128)(2,1)}, bf16[2,1024,384]{2,1,0:T(8,128)(2,1)}) custom-call(s32[2]{0:T(128)} %compare_convert_fusion.moved, bf16[16,2,48,1024]{3,2,1,0:T(8,128)(2,1)} %bitcast.15, bf16[16,2,48,1024]{3,2,1,0:T(8,128)(2,1)} %bitcast.16, ...), custom_call_target="tpu_custom_call" | custom-call | tf_op jit(solution)/shard_map/experts/pallas_call | solution.py:332
  151.2 89.7 %combine.1 = (bf16[128,1024]{1,0:T(8,128)(2,1)S(1)}, bf16[128,1024]{1,0:T(8,128)(2,1)S(1)}, bf16[3,2,256,768]{3,2,1,0:T(8,128)(2,1)}, bf16[3,2,256,384]{3,2,1,0:T(8,128)(2,1)S(1)}) custom-call(bf16[16,96,1024]{2,1,0:T(8,128)(2,1)} %bitcast.13, bf16[16,96,1024]{2,1,0:T(8,128)(2,1)} %bitcast.14, bf16[2,768,512]{2,1,0:T(8,128)(2,1)S(1)} %get-tuple-element.26.pick, ...), custom_call_target="tpu_custom_call" | custom-call | tf_op jit(solution)/shard_map/combine/pallas_call | solution.py:491
  240.9 0.0 copy-start.7
  240.9 0.2 convert_reduce_fusion.1
  241.1 2.1 convert_add_fusion.1
  243.2 0.0 copy-done.7
  243.2 0.4 convert_reduce_fusion
  243.5 2.5 %convert_add_fusion = f32[2,256,768]{2,1,0:T(8,128)} fusion(f32[2,256,768]{2,1,0:T(8,128)S(1)} %convert_reduce_fusion, bf16[2,1024,768]{2,1,0:T(8,128)(2,1)} %get-tuple-element.28.g_gu, s32[]{:T(128)S(6)} %select_n.25), kind=kLoop, calls=%fused_computation.2 | loop fusion | flops 786432 | bytes 3932164 | tf_op jit(solution)/shard_map/add | solution.py:534
  246.0 0.7 copy.16
  246.7 0.7 copy.17
Async XLA Ops:
  8.0 1.0 copy-start.1
  9.0 0.9 copy-start.2
  9.9 0.9 copy-start.3
  10.9 0.9 copy-start.4
  11.8 0.7 copy-start.5
  12.5 0.7 copy-start.6
  123.3 0.9 copy-start
  240.9 2.3 copy-start.7

commit v2 on v0

v2 whole, which is shorter than its diff:
```python
import jax
import jax.numpy as jnp
from jax import lax
from jax.experimental import pallas as pl
from jax.experimental.pallas import tpu as pltpu
from jax.sharding import PartitionSpec as P

MESH = pl.DeviceIdType.MESH
bf16, f32 = jnp.bfloat16, jnp.float32

grad_scale = 0.0625
PLANE = 8
CAP = 12
BLOCKS = 4
ROWS = CAP * BLOCKS
SLOTS = 2
GROUPS = ((0, 1, -1, -2), (2, 3, -3, 4))
PLACE = {offset: g * BLOCKS + b for g, group in enumerate(GROUPS) for b, offset in enumerate(group)}
HOPS = [(k - 1, k, -1) for k in range(1, 5)] + [(1 - k, -k, 1) for k in range(1, 4)]
BACK = (3, 2, 1, 4, -3, -2, -1)
TILE = 256


def dot_nn(a, b):
    return lax.dot_general(a, b, (((1,), (0,)), ((), ())), preferred_element_type=f32)


def dot_nt(a, b):
    return lax.dot_general(a, b, (((1,), (1,)), ((), ())), preferred_element_type=f32)


def dot_tn(a, b):
    return lax.dot_general(a, b, (((0,), (0,)), ((), ())), preferred_element_type=f32)


def remote(src, dst, send, recv, device):
    return pltpu.make_async_remote_copy(
        src_ref=src, dst_ref=dst, send_sem=send, recv_sem=recv, device_id=device, device_id_type=MESH
    )


def layer_kernel(
    tokens, routes_t, gates_t, cot, partner, w_gu, w_dn,
    mixed, grad_tokens, own_gu, own_dn, xr_gu, xr_dn,
    tok_v, cot_v, routes_v, gates_v, partner_v,
    xt, xc, rg, pick, pick_gate, out_t, out_c, got_t, got_c,
    gu, dn, ws_gu, ws_dn, wr_gu, wr_dn,
    pre, hid, gpre, g_gu, g_dn, ybuf, part, ring_in,
    load_sem, t_send, t_recv, r_send, r_recv, y_send, y_recv, l_sem, w_send, w_recv, v_send, v_recv,
    b_send, b_recv, bl_sem, z_send, z_recv, x_send, x_recv, own_sem,
):
    dp, index = lax.axis_index("dp"), lax.axis_index("expert")
    n_dp, n_z = lax.axis_size("dp"), lax.axis_size("expert") // PLANE
    z, yc = index // PLANE, index % PLANE
    count, width = tokens.shape
    half = width // 2
    ff = dn.shape[2]
    n_slots = lax.axis_size("expert") * SLOTS
    picked = PLANE * SLOTS * ROWS
    quarter = width // n_dp

    def at_z(shift):
        return (dp, lax.rem(z + shift + n_z, n_z) * PLANE + yc)

    def at_yc(shift):
        return (dp, z * PLANE + lax.rem(yc + shift, PLANE))

    def at_x(shift):
        return (lax.rem(dp + shift, n_dp), z * PLANE + yc)

    loads = [
        pltpu.make_async_copy(src, dst, load_sem.at[n])
        for n, (src, dst) in enumerate(
            (
                (tokens, tok_v), (routes_t, routes_v), (gates_t, gates_v), (partner, partner_v),
                (cot, cot_v), (w_gu, gu), (w_dn, dn),
            )
        )
    ]
    for load in loads:
        load.start()

    barrier = pltpu.get_barrier_semaphore()
    peers = [at_z(1), at_z(-1), at_z(n_z // 2)]
    peers += [at_yc(i) for i in range(1, PLANE)] + [at_x(i) for i in range(1, 4)]
    for device in peers:
        pl.semaphore_signal(barrier, inc=1, device_id=device, device_id_type=MESH)
    pl.semaphore_wait(barrier, len(peers))

    def rows_of(s):
        return (xt, xc)[s // 2].at[s % 2]

    def hop(s, n):
        here, there, way = HOPS[n]
        buf = rows_of(s)
        return remote(buf.at[PLACE[here]], buf.at[PLACE[there]], t_send.at[s, n], t_recv.at[s, n], at_z(way))

    def r_hop(n):
        here, there, way = HOPS[n]
        return remote(rg.at[PLACE[here]], rg.at[PLACE[there]], r_send.at[n], r_recv.at[n], at_z(way))

    for n in range(4):
        loads[n].wait()
    for h in range(2):
        xt[h, 0] = tok_v[:, h * half : (h + 1) * half]
        hop(h, 0).start()
        hop(h, 4).start()

    row = lax.broadcasted_iota(jnp.int32, (n_slots, count), 0)
    col = lax.broadcasted_iota(jnp.int32, (n_slots, count), 1)
    named = jnp.zeros((n_slots, count), f32)
    weight = jnp.zeros((n_slots, count), f32)
    for k in range(routes_t.shape[0]):
        hit = routes_v[k : k + 1, :] == row
        named = named + jnp.where(hit, 1.0, 0.0)
        weight = weight + jnp.where(hit, gates_v[k : k + 1, :], 0.0)
    to_slot = jnp.where(partner_v[...] == row, 1.0, 0.0).astype(bf16)
    named = dot_tn(to_slot, named.astype(bf16))
    weight = dot_tn(to_slot, weight.astype(bf16))
    upto = jnp.where(row <= col, 1.0, 0.0).astype(bf16)
    rank = named * dot_nn(named.astype(bf16), upto)
    rg[0, :n_slots, :] = rank.astype(bf16)
    rg[0, n_slots:, :] = weight.astype(bf16)
    r_hop(0).start()
    r_hop(4).start()

    lane = lax.broadcasted_iota(jnp.int32, (1, n_slots), 1)
    moved = []
    for j in range(SLOTS):
        held = jnp.where(lane == index * SLOTS + j, partner_v[...], 0)
        held = jnp.sum(held.astype(f32), axis=1, keepdims=True)
        first = (index * SLOTS).astype(f32)
        moved.append((held < first) | (held > first + (SLOTS - 1)))

    loads[4].wait()
    for h in range(2):
        xc[h, 0] = cot_v[:, h * half : (h + 1) * half]
    loads[5].wait()
    loads[6].wait()
    mine = pl.ds(pl.multiple_of(dp * quarter, quarter), quarter)
    ws_gu[...] = jnp.where(moved[1], gu[1, mine, :], gu[0, mine, :])
    ws_dn[...] = jnp.where(moved[1], dn[1, mine, :], dn[0, mine, :])

    number = lax.broadcasted_iota(jnp.int32, (picked, 1), 0).astype(f32)
    slot_of = jnp.floor((number + 0.5) * (1.0 / ROWS))
    rest = number - ROWS * slot_of
    block_of = jnp.floor((rest + 0.5) * (1.0 / CAP))
    rank_of = rest - CAP * block_of + 1.0
    per_plane = PLANE * SLOTS
    slot_lane = lax.broadcasted_iota(jnp.int32, (picked, per_plane), 1).astype(f32)
    expand = jnp.where(slot_lane == slot_of, 1.0, 0.0).astype(bf16)

    def build(g):
        for b in range(BLOCKS):
            start = pl.multiple_of(z * per_plane, per_plane)
            ranks = rg[g * BLOCKS + b, pl.ds(start, per_plane), :]
            gates = rg[g * BLOCKS + b, pl.ds(n_slots + start, per_plane), :]
            hit = dot_nn(expand, ranks) == jnp.where(block_of == b, rank_of, -1.0)
            spread = dot_nn(expand, gates)
            columns = slice(b * count, (b + 1) * count)
            pick[g, :, columns] = jnp.where(hit, 1.0, 0.0).astype(bf16)
            pick_gate[g, :, columns] = jnp.where(hit, spread, 0.0).astype(bf16)

    def out_of(s):
        return (out_t, out_c)[s // 2]

    def got_of(s):
        return (got_t, got_c)[s // 2]

    def y_copy(s, g, i):
        p = lax.rem(yc + i, PLANE)
        n = 2 * s + g
        return remote(
            out_of(s).at[s % 2, g, p], got_of(s).at[s % 2, g, yc], y_send.at[n, i], y_recv.at[n, i], at_yc(i)
        )

    def y_local(s, g):
        return pltpu.make_async_copy(
            out_of(s).at[s % 2, g, yc], got_of(s).at[s % 2, g, yc], l_sem.at[2 * s + g]
        )

    def send_rows(s, g):
        matrix, buf, out = (pick, pick_gate)[s // 2], (xt, xc)[s // 2], out_of(s)

        @pl.loop(0, half // TILE)
        def _(j):
            columns = pl.ds(pl.multiple_of(j * TILE, TILE), TILE)
            block = buf[s % 2, g * BLOCKS : (g + 1) * BLOCKS, :, columns].reshape(BLOCKS * count, TILE)
            rows = dot_nn(matrix[g], block).astype(bf16)
            out[s % 2, g, :, :, columns] = rows.reshape(PLANE, SLOTS * ROWS, TILE)

        for i in range(1, PLANE):
            y_copy(s, g, i).start()
        y_local(s, g).start()

    def rows_arrived(s, g):
        for i in range(1, PLANE):
            y_copy(s, g, i).wait_recv()
        y_local(s, g).wait()

    def rows_left(s, g):
        for i in range(1, PLANE):
            y_copy(s, g, i).wait_send()

    def ring(s, k, follow=True):
        hop(s, k - 1).wait_recv()
        if k < 4:
            hop(s, k + 3).wait_recv()
        if k < 4:
            hop(s, k).start()
        if k < 3:
            hop(s, k + 4).start()

    def r_ring(k):
        r_hop(k - 1).wait_recv()
        if k < 4:
            r_hop(k + 3).wait_recv()
            r_hop(k).start()
        if k < 3:
            r_hop(k + 4).start()

    traded = ((ws_gu, wr_gu), (ws_dn, wr_dn))

    def w_copy(n):
        return remote(traded[n][0], traded[n][1].at[mine, :], w_send.at[n], w_recv.at[n], at_z(n_z // 2))

    def v_copy(n, i):
        here = traded[n][1].at[mine, :]
        return remote(here, here, v_send.at[n, i], v_recv.at[n, i], at_x(i))

    ring(0, 1)
    r_ring(1)
    ring(1, 1)
    ring(0, 2)
    r_ring(2)
    build(0)
    send_rows(0, 0)
    ring(1, 2)
    send_rows(1, 0)
    ring(0, 3)
    r_ring(3)
    ring(1, 3)
    for s in (2, 3):
        hop(s, 0).start()
        hop(s, 4).start()
    w_copy(0).start()
    w_copy(1).start()
    ring(0, 4)
    r_ring(4)
    build(1)
    send_rows(0, 1)
    ring(1, 4)
    send_rows(1, 1)
    ring(2, 1)
    ring(3, 1)
    ring(2, 2)
    ring(3, 2)
    send_rows(2, 0)
    send_rows(3, 0)
    ring(2, 3)
    ring(3, 3)
    ring(2, 4)
    send_rows(2, 1)
    ring(3, 4)
    send_rows(3, 1)
    for n in range(2):
        w_copy(n).wait_recv()
        for i in range(1, 4):
            v_copy(n, i).start()
    for n in range(2):
        for i in range(1, 4):
            v_copy(n, i).wait_recv()

    @pl.loop(0, width // TILE)
    def _(i):
        rows = pl.ds(pl.multiple_of(i * TILE, TILE), TILE)
        for j in range(SLOTS):
            gu[j, rows, :] = jnp.where(moved[j], wr_gu[rows, :], gu[j, rows, :])
            dn[j, rows, :] = jnp.where(moved[j], wr_dn[rows, :], dn[j, rows, :])

    many = PLANE * ROWS

    def b_copy(s, g, i):
        p = lax.rem(yc + i, PLANE)
        n = 2 * s + g
        return remote(
            out_of(s).at[s % 2, g, p], ybuf.at[n, yc], b_send.at[n, i], b_recv.at[n, i], at_yc(i)
        )

    def b_local(s, g):
        return pltpu.make_async_copy(out_of(s).at[s % 2, g, yc], ybuf.at[2 * s + g, yc], bl_sem.at[2 * s + g])

    def b_start(s, g):
        for i in range(1, PLANE):
            b_copy(s, g, i).start()
        b_local(s, g).start()

    def slot_rows(buf, h, g, j):
        return buf[h, g, :, j * ROWS : (j + 1) * ROWS, :].reshape(many, half)

    def put_rows(buf, h, g, j, value):
        buf[h, g, :, j * ROWS : (j + 1) * ROWS, :] = value.astype(bf16).reshape(PLANE, ROWS, half)

    for s in range(2):
        for g in range(2):
            rows_arrived(s, g)
            rows_left(s, g)
    for g in (1, 0):
        for j in range(SLOTS):
            x = slot_rows(got_t, 0, g, j)
            first = dot_nn(x, gu[j, :half, :])
            x = slot_rows(got_t, 1, g, j)
            both = first + dot_nn(x, gu[j, half:, :])
            pre[j, g] = both
            gate, up = both[:, :ff], both[:, ff:]
            hidden = (gate * jax.nn.sigmoid(gate) * up).astype(bf16)
            hid[j, g] = hidden
            for h in range(2):
                put_rows(out_t, h, g, j, dot_nt(hidden, dn[j, h * half : (h + 1) * half, :]))
        for s in range(2):
            b_start(s, g)

    for g in (0, 1):
        for s in (2, 3):
            rows_arrived(s, g)
            rows_left(s, g)
        for j in range(SLOTS):
            c = slot_rows(got_c, 0, g, j)
            first = dot_nn(c, dn[j, :half, :])
            c = slot_rows(got_c, 1, g, j)
            grad = first + dot_nn(c, dn[j, half:, :])
            gate, up = pre[j, g, :, :ff], pre[j, g, :, ff:]
            sig = jax.nn.sigmoid(gate)
            gpre[j, g, :, :ff] = (grad * up * sig * (1.0 + gate * (1.0 - sig))).astype(bf16)
            gpre[j, g, :, ff:] = (grad * (gate * sig)).astype(bf16)
            for h in range(2):
                put_rows(out_c, h, g, j, dot_nt(gpre[j, g], gu[j, h * half : (h + 1) * half, :]))
    for g in (1, 0):
        for s in (2, 3):
            b_start(s, g)

    for j in range(SLOTS):
        for h in range(2):

            @pl.loop(0, half // TILE)
            def _(i):
                columns = pl.ds(pl.multiple_of(i * TILE, TILE), TILE)
                to = pl.ds(pl.multiple_of(h * half + i * TILE, TILE), TILE)
                block = slice(j * ROWS, (j + 1) * ROWS)
                x = got_t[h, :, :, block, columns].reshape(2 * many, TILE)
                g_gu[j, to, :] = (dot_tn(x, gpre[j].reshape(2 * many, 2 * ff)) * grad_scale).astype(bf16)
                c = got_c[h, :, :, block, columns].reshape(2 * many, TILE)
                g_dn[j, to, :] = (dot_tn(c, hid[j].reshape(2 * many, ff)) * grad_scale).astype(bf16)

    grads = ((g_gu, xr_gu, own_gu), (g_dn, xr_dn, own_dn))

    def x_copy(n, i):
        to = lax.rem(dp + i, n_dp)
        rows = pl.ds(pl.multiple_of(to * quarter, quarter), quarter)
        return remote(
            grads[n][0].at[:, rows, :], grads[n][1].at[i - 1], x_send.at[n, i], x_recv.at[n, i], at_x(i)
        )

    def own_copy(n):
        return pltpu.make_async_copy(grads[n][0].at[:, mine, :], grads[n][2], own_sem.at[n])

    for n in range(2):
        for i in range(1, 4):
            x_copy(n, i).start()
        own_copy(n).start()

    for s in range(4):
        for n in range(7):
            hop(s, n).wait_send()

    def combine(s, g):
        for i in range(1, PLANE):
            b_copy(s, g, i).wait_recv()
        b_local(s, g).wait()
        matrix = (pick_gate, pick)[s // 2]

        @pl.loop(0, half // TILE)
        def _(j):
            columns = pl.ds(pl.multiple_of(j * TILE, TILE), TILE)
            y = ybuf[2 * s + g, :, :, columns].reshape(picked, TILE)
            part[s % 2, g, :, columns] = dot_tn(matrix[g], y)

    def own_part(s, offset):
        g, b = PLACE[offset] // BLOCKS, PLACE[offset] % BLOCKS
        return part[s % 2, g, b * count : (b + 1) * count, :]

    def z_copy(s, n):
        way = 1 if n < 3 else -1
        return remote(rows_of(s).at[n], ring_in.at[s, n], z_send.at[s, n], z_recv.at[s, n], at_z(way))

    def z_step(s, n):
        total = own_part(s, BACK[n])
        if n not in (0, 3):
            z_copy(s, n - 1).wait_recv()
            total = total + ring_in[s, n - 1].astype(f32)
        rows_of(s)[n] = total.astype(bf16)
        z_copy(s, n).start()

    def finish(s):
        z_copy(s, 2).wait_recv()
        z_copy(s, 6).wait_recv()
        total = own_part(s, 0) + ring_in[s, 2].astype(f32) + ring_in[s, 6].astype(f32)
        to = slice(s % 2 * half, (s % 2 + 1) * half)
        (mixed, grad_tokens)[s // 2][:, to] = total.astype(bf16)

    for pair in ((0, 1), (2, 3)):
        for s in pair:
            combine(s, 1)
            z_step(s, 0)
            z_step(s, 3)
        for s in pair:
            z_step(s, 1)
            z_step(s, 4)
        for s in pair:
            combine(s, 0)
            z_step(s, 2)
            z_step(s, 5)
        for s in pair:
            z_step(s, 6)
        for s in pair:
            finish(s)

    for n in range(7):
        r_hop(n).wait_send()
        for s in range(4):
            z_copy(s, n).wait_send()
    for s in range(4):
        for g in range(2):
            for i in range(1, PLANE):
                b_copy(s, g, i).wait_send()
    for n in range(2):
        w_copy(n).wait_send()
        own_copy(n).wait()
        for i in range(1, 4):
            v_copy(n, i).wait_send()
            x_copy(n, i).wait_send()
            x_copy(n, i).wait_recv()


def layer(tokens, routes, gates, cotangent, partner, w_gu, w_dn):
    count, width = tokens.shape
    slots, _, ff2 = w_gu.shape
    ff, half = ff2 // 2, width // 2
    n_dp, n_slots = lax.axis_size("dp"), lax.axis_size("expert") * slots
    quarter = width // n_dp
    picked = PLANE * SLOTS * ROWS
    vmem, hbm = pl.BlockSpec(memory_space=pltpu.VMEM), pl.BlockSpec(memory_space=pl.ANY)
    dma = pltpu.SemaphoreType.DMA
    many = PLANE * ROWS
    shape = jax.ShapeDtypeStruct
    return pl.pallas_call(
        layer_kernel,
        out_shape=(
            shape((count, width), bf16), shape((count, width), bf16),
            shape((slots, quarter, ff2), bf16), shape((slots, quarter, ff), bf16),
            shape((n_dp - 1, slots, quarter, ff2), bf16), shape((n_dp - 1, slots, quarter, ff), bf16),
        ),
        in_specs=[hbm] * 7,
        out_specs=(vmem, vmem, hbm, hbm, hbm, hbm),
        scratch_shapes=[
            pltpu.VMEM((count, width), bf16), pltpu.VMEM((count, width), bf16),
            pltpu.VMEM(routes.shape[::-1], jnp.int32), pltpu.VMEM(gates.shape[::-1], f32),
            pltpu.VMEM((1, n_slots), jnp.int32),
            pltpu.VMEM((2, 2 * BLOCKS, count, half), bf16), pltpu.VMEM((2, 2 * BLOCKS, count, half), bf16),
            pltpu.VMEM((2 * BLOCKS, 2 * n_slots, count), bf16),
            pltpu.VMEM((2, picked, BLOCKS * count), bf16), pltpu.VMEM((2, picked, BLOCKS * count), bf16),
            pltpu.VMEM((2, 2, PLANE, SLOTS * ROWS, half), bf16),
            pltpu.VMEM((2, 2, PLANE, SLOTS * ROWS, half), bf16),
            pltpu.VMEM((2, 2, PLANE, SLOTS * ROWS, half), bf16),
            pltpu.VMEM((2, 2, PLANE, SLOTS * ROWS, half), bf16),
            pltpu.VMEM((slots, width, ff2), bf16), pltpu.VMEM((slots, width, ff), bf16),
            pltpu.VMEM((quarter, ff2), bf16), pltpu.VMEM((quarter, ff), bf16),
            pltpu.VMEM((width, ff2), bf16), pltpu.VMEM((width, ff), bf16),
            pltpu.VMEM((slots, 2, many, ff2), f32),
            pltpu.VMEM((slots, 2, many, ff), bf16), pltpu.VMEM((slots, 2, many, ff2), bf16),
            pltpu.VMEM((slots, width, ff2), bf16), pltpu.VMEM((slots, width, ff), bf16),
            pltpu.VMEM((8, PLANE, SLOTS * ROWS, half), bf16),
            pltpu.VMEM((2, 2, BLOCKS * count, half), f32),
            pltpu.VMEM((4, 7, count, half), bf16),
            dma((7,)), dma((4, 7)), dma((4, 7)), dma((7,)), dma((7,)),
            dma((8, PLANE)), dma((8, PLANE)), dma((8,)), dma((2,)), dma((2,)), dma((2, 4)), dma((2, 4)),
            dma((8, PLANE)), dma((8, PLANE)), dma((8,)), dma((4, 7)), dma((4, 7)), dma((2, 4)), dma((2, 4)),
            dma((2,)),
        ],
        compiler_params=pltpu.CompilerParams(
            collective_id=0, has_side_effects=True, vmem_limit_bytes=62 << 20
        ),
        name="layer",
    )(tokens, routes.T, gates.T, cotangent, partner[None, :], w_gu, w_dn)


def local(*args):
    mixed, grad_tokens, own_gu, own_dn, xr_gu, xr_dn = layer(*args)

    def total(own, others):
        return own.astype(f32) + jnp.sum(others.astype(f32), axis=0)

    return mixed, grad_tokens, total(own_gu, xr_gu), total(own_dn, xr_dn)


def solution(mesh):
    token_spec = P(("dp", "expert"), None)
    weight_spec = P("expert", None, None)
    grad_spec = P("expert", "dp", None)
    return jax.shard_map(
        local,
        mesh=mesh,
        in_specs=(token_spec, token_spec, token_spec, token_spec, P(None), weight_spec, weight_spec),
        out_specs=(token_spec, token_spec, grad_spec, grad_spec),
        check_vma=False,
    )
```

time: 639 us -> 210 us (0.33); the launches traced: 631 us -> 209 us
  starting transfers between devices: 238 us -> 0 us
  waiting for transfers between devices: 205 us -> 0 us
  Pallas kernels: 0 us -> 202 us
  local copies, waits for them, and re-layouts: 99.3 us -> 2.2 us
  matrix products: 43.6 us -> 0 us
  other arithmetic: 30.2 us -> 4.25 us
  between operations: 14.6 us -> 0.68 us
    all_to_all x4 -> x0, starting transfers between devices: 232 us -> none  [the longest x1 208 us: local(): lax.all_to_all(grad_pad[filler].reshape(buffer_shape), 'expert', split_ax...]
    all_to_all x4 -> x0, waiting for transfers between devices: 205 us -> none  [the longest x1 63.5 us: local(): lax.all_to_all(expert_out, 'expert', split_axis=0, concat_axis=0, tiled=T...]
    pallas_call x0 -> x1, Pallas kernels: none -> 202 us  [layer(): pl.pallas_call(layer_kernel, out_shape=(shape((count, width), bf16), shap...]
    dot_general x7 -> x0, matrix products: 43.6 us -> none  [the longest x1 14.3 us: local(): jnp.einsum('sjcd,sjcf->jdf', arrived, grad_pre, preferred_element_type=jn...]
    reshape x6 -> x0, local copies, waits for them, and re-layouts: 32.5 us -> none  [the longest x2 13.2 us: local(): grad_pad[filler].reshape(buffer_shape)]
    gather x6 -> x0, local copies, waits for them, and re-layouts: 30.6 us -> none  [the longest x2 9.07 us: pick_slots(): return jnp.take(stacked, index, axis=0)]
    concatenate x2 -> x0, other arithmetic: 10.5 us -> none  [pick_slots(): stacked = jnp.concatenate([own_slots, received], axis=0)]
    convert_element_type x2 -> x0, local copies, waits for them, and re-layouts: 9.83 us -> none  [the longest x1 4.93 us: local(): expert_out = jnp.einsum('sjcf,jdf->sjcd', hidden, weight_dn, preferred_el...]
  transfers between devices with their start and end apart: 6 -> 0, of which waited for: 4 -> 0; matrix products, arithmetic and copies ran while one was open for 17% -> 0% of each run, Pallas kernels for 0% -> 0%
where the time goes in v2:
time: 210 us; the launch traced here: 209 us
  Pallas kernels  202 us (96%)
  other arithmetic  4.25 us (2%)
  local copies, waits for them, and re-layouts  2.2 us (1%)
    pallas_call x1, Pallas kernels, layer(): pl.pallas_call(layer_kernel, out_shape=(shape((count, width), bf16), shap...  202 us

profile of v2, /device:TPU:2, one launch (start us, length us, event | category | flops | bytes accessed | tf_op | source)
XLA Modules:
  0.0 209.0 jit_solution(11031513426715291416)
XLA Ops:
  0.6 201.8 %layer.1 = (bf16[128,1024]{1,0:T(8,128)(2,1)}, bf16[128,1024]{1,0:T(8,128)(2,1)}, bf16[2,256,768]{2,1,0:T(8,128)(2,1)}, bf16[2,256,384]{2,1,0:T(8,128)(2,1)}, bf...) custom-call(bf16[128,1024]{1,0:T(8,128)(2,1)} %tokens.1, s32[8,128]{1,0:T(8,128)} %bitcast.3, ...), custom_call_target="tpu_custom_call" | custom-call | tf_op jit(solution)/shard_map/layer/pallas_call | solution.py:456
  202.5 0.0 copy-start.2
  202.5 0.0 copy-start
  202.5 1.7 convert_reduce_fusion.1
  204.2 0.0 copy-done.2
  204.2 0.9 convert_add_fusion.1
  205.1 0.0 copy-done
  205.1 0.0 copy-start.1
  205.1 0.4 convert_reduce_fusion
  205.5 0.8 copy-done.1
  206.2 0.0 copy-start.4
  206.3 0.0 copy-start.3
  206.3 1.3 convert_add_fusion
  207.5 0.0 copy-done.4
  207.5 0.7 copy.13
  208.2 0.0 copy-done.3
  208.3 0.7 copy.14
Async XLA Ops:
  202.5 1.7 copy-start.2
  202.5 2.6 %copy-start = (bf16[3,2,256,768]{3,2,1,0:T(8,128)(2,1)S(1)}, bf16[3,2,256,768]{3,2,1,0:T(8,128)(2,1)}, u32[]{:S(2)}) copy-start(bf16[3,2,256,768]{3,2,1,0:T(8,128)(2,1)} %get-tuple-element.13) | copy-start | bytes 7077892
  205.1 1.1 copy-start.1
  206.2 1.3 copy-start.4
  206.3 2.0 copy-start.3
